TPU v7x, 32 devices: a whole 2x2x4 slice. The times are simulated.
32 devices in a mesh: tm: 8 (over z, core), space: 2 (over x), samples: 2 (over y).
Axes of the slice: x: 2, y: 2, z: 4, core: 2. Of those that a mesh axis runs over, the one named last changes fastest.
Arguments:
- fields: bfloat16 [2, 16, 16, 128, 256], P('samples', 'tm', 'space'), may hold values from -6 to 6
- out_grad: bfloat16 [2, 16, 16, 128, 256], P('samples', 'tm', 'space'), may hold values from -6 to 6
- spatial_weight: bfloat16 [3, 3, 256, 256], replicated, may hold values from -0.125 to 0.125
- temporal_weight: bfloat16 [5, 256, 256], replicated, may hold values from -0.15625 to 0.15625
Outputs:
- block_out: bfloat16 [2, 16, 16, 128, 256], P('samples', 'tm', 'space')
- fields_grad: bfloat16 [2, 16, 16, 128, 256], P('samples', 'tm', 'space')
- spatial_grad: float32 [3, 3, 256, 256], replicated
- temporal_grad: float32 [5, 256, 256], replicated
All inputs are finite; a program needn't handle non-finite values.
Results may differ from a plain program's by a relative error of at most 0.012.
Values may be sent and summed in bfloat16 or wider, within the bound.
A program may use at most 128 MiB of HBM per device.

v0:
```python
import jax
import jax.numpy as jnp
from jax import lax
from jax.sharding import PartitionSpec as P


def padded_2(shard, sides, width, wrap):
    for axis, dim in sides:
        peers, length = (lax.axis_size(axis), shard.shape[dim])
        up = [(i, (i + 1) % peers) for i in range(peers if wrap else peers - 1)]
        down = [(j, i) for i, j in up]
        last = lax.slice_in_dim(shard, length - width, length, axis=dim)
        first = lax.slice_in_dim(shard, 0, width, axis=dim)
        before = lax.ppermute(last, axis, up)
        after = lax.ppermute(first, axis, down)
        shard = jnp.concatenate([before, shard, after], axis=dim)
    return shard


def gelu_tanh(value):
    return jax.nn.gelu(value, approximate=True)


def pad_cells(field):
    return jnp.pad(field, ((0, 0), (0, 0), (0, 0), (1, 1), (0, 0)))


def spatial_apply(padded, weight, offset, transpose):
    shape = padded.shape
    rows = shape[2] - 2
    cells = shape[3] - 2
    chans = shape[4]
    total = jnp.zeros((shape[0], shape[1], rows, cells, chans), jnp.float32)
    for i in range(3):
        for j in range(3):
            si = offset - i if transpose else i
            sj = offset - j if transpose else j
            piece = padded[:, :, si : si + rows, sj : sj + cells, :].reshape(-1, chans)
            tap = weight[i, j].T if transpose else weight[i, j]
            total = total + jnp.dot(piece, tap, preferred_element_type=jnp.float32).reshape(
                total.shape
            )
    return total


def temporal_apply(act_pad, grad_pad, weight, nframes):
    chans = act_pad.shape[4]
    shape = (act_pad.shape[0], nframes) + act_pad.shape[2:]
    middle = grad_pad[:, 2 : 2 + nframes].reshape(-1, chans)
    block = jnp.zeros(shape, jnp.float32)
    act_grad = jnp.zeros(shape, jnp.float32)
    sums = []
    for k in range(5):
        shifted = act_pad[:, k : k + nframes].reshape(-1, chans)
        block = block + jnp.dot(shifted, weight[k], preferred_element_type=jnp.float32).reshape(
            shape
        )
        sums.append(jnp.dot(shifted.T, middle, preferred_element_type=jnp.float32))
        back = grad_pad[:, 4 - k : 4 - k + nframes].reshape(-1, chans)
        act_grad = act_grad + jnp.dot(
            back, weight[k].T, preferred_element_type=jnp.float32
        ).reshape(shape)
    return (block.astype(jnp.bfloat16), act_grad.astype(jnp.bfloat16), jnp.stack(sums))


def shards(fields, out_grad, spatial_weight, temporal_weight):
    chans = fields.shape[4]
    padded = pad_cells(padded_2(fields, (("space", 2),), 1, True))
    hidden = spatial_apply(padded, spatial_weight, 0, False)
    act = gelu_tanh(hidden).astype(jnp.bfloat16)
    stacked = jnp.stack([act, out_grad])
    margined = padded_2(stacked, (("tm", 2),), 2, False)
    block_out, act_grad, temporal_sum = temporal_apply(
        margined[0], margined[1], temporal_weight, act.shape[1]
    )
    _, pullback = jax.vjp(gelu_tanh, hidden)
    hidden_grad = pullback(act_grad.astype(jnp.float32))[0].astype(jnp.bfloat16)
    rows_hg = hidden_grad.reshape(-1, chans)
    height = fields.shape[2]
    wide = fields.shape[3]
    spatial_list = []
    for i in range(3):
        for j in range(3):
            piece = padded[:, :, i : i + height, j : j + wide, :].reshape(-1, chans)
            spatial_list.append(jnp.dot(piece.T, rows_hg, preferred_element_type=jnp.float32))
    spatial_sum = jnp.stack(spatial_list).reshape(3, 3, chans, chans)
    grad_padded = pad_cells(padded_2(hidden_grad, (("space", 2),), 1, True))
    fields_grad = spatial_apply(grad_padded, spatial_weight, 2, True).astype(jnp.bfloat16)
    all_rows = (
        fields.shape[0]
        * fields.shape[1]
        * height
        * wide
        * lax.axis_size("tm")
        * lax.axis_size("space")
        * lax.axis_size("samples")
    )
    factor = all_rows ** (-0.5)
    spatial_total, temporal_total = lax.psum(
        (spatial_sum, temporal_sum), ("tm", "space", "samples")
    )
    return (block_out, fields_grad, spatial_total * factor, temporal_total * factor)


def solution(mesh):
    return jax.shard_map(
        shards,
        mesh=mesh,
        in_specs=(
            P("samples", "tm", "space", None, None),
            P("samples", "tm", "space", None, None),
            P(),
            P(),
        ),
        out_specs=(
            P("samples", "tm", "space", None, None),
            P("samples", "tm", "space", None, None),
            P(),
            P(),
        ),
        check_vma=False,
    )
```

profile of v0, /device:TPU:0, one launch (start us, length us, event | category | flops | bytes accessed | tf_op | source)
XLA Modules:
  0.0 237.6 jit_solution(12061235643872717782)
XLA Ops:
  7.2 1.0 fusion.130
  8.2 3.0 %collective-permute-start = (bf16[1,2,1,128,256]{4,3,2,1,0:T(8,128)(2,1)S(1)}, bf16[1,2,1,128,256]{4,3,2,1,0:T(8,128)(2,1)S(1)}, u32[]{:S(2)}, u32[]{:S(2)}) collective-permute-start(bf16[1,2,1,128,256]{4,3,2,1,0:T(8,128)(2,1)S(1)} %get-tuple-element.10), channel_id=1, source_target_pairs={{0,2},{2,0},{1,3},{3,1},{4,6},{6,4},{5,7},{7,5},{8,10},{10,8},{9,1... | collective-permute-start | bytes 393224 | tf_op jit(solution)/shard_map/ppermute | solution.py:14
  11.3 1.7 fusion.47
  13.1 2.5 %collective-permute-done = bf16[1,2,1,128,256]{4,3,2,1,0:T(8,128)(2,1)S(1)} collective-permute-done((bf16[1,2,1,128,256]{4,3,2,1,0:T(8,128)(2,1)S(1)}, bf16[1,2,1,128,256]{4,3,2,1,0:T(8,128)(2,1)S(1)}, u32[]{:S(2)}, u32[]{:S(2)}) %collective-permute-start) | collective-permute-done | bytes 131104 | tf_op jit(solution)/shard_map/ppermute | solution.py:14
  15.6 2.0 collective-permute-done.1
  17.5 0.7 select_maximum_fusion.2
  18.3 0.4 fusion.54
  18.7 0.5 fusion.53
  19.2 0.4 fusion.52
  19.6 0.5 fusion.51
  20.0 0.4 fusion.50
  20.5 0.5 fusion.55
  20.9 0.4 fusion.61
  21.4 1.4 add_add_fusion
  22.7 0.7 fusion.49
  23.4 0.6 copy-done.3
  24.1 1.3 collective-permute-start.3
  25.4 3.3 %collective-permute-start.2 = (bf16[2,1,2,8,128,256]{5,4,3,2,1,0:T(8,128)(2,1)S(1)}, bf16[2,1,2,8,128,256]{5,4,3,2,1,0:T(8,128)(2,1)S(1)}, u32[]{:S(2)}, u32[]{:S(2)}) collective-permute-start(bf16[2,1,2,8,128,256]{5,4,3,2,1,0:T(8,128)(2,1)S(1)} %pad_maximum_fusion.1), channel_id=1, source_target_pairs={{0,4},{4,8},{8,12},{12,16},{16,20},{20,24},{24,28},{1,5},{5,9},{9,... | collective-permute-start | bytes 6291464 | tf_op jit(solution)/shard_map/ppermute | solution.py:14
  28.8 1.4 collective-permute-done.3
  30.2 2.1 collective-permute-done.2
  32.3 3.9 %pad_maximum_fusion = bf16[2,1,6,8,128,256]{5,4,3,2,1,0:T(8,128)(2,1)S(1)} fusion(bf16[2,1,2,8,128,256]{5,4,3,2,1,0:T(8,128)(2,1)S(1)} %collective-permute-done.3, bf16[1,1,2,8,128,256]{5,4,3,2,1,0:T(8,128)(2,1)S(1)} %bitcast.367, bf16[1,1,2,8,128,256]{5,4,3,2,1,0:T(8,128)(2,1)S(1)} %fusion.49, bf16[2,1,2,8,128,256]{5,4,3,2,1,0:T(8,128)(2,1)S(1)} %collective-permute-done.2), kind=kLoop, calls=%fused_computation | loop fusion | flops 9437184 | bytes 12582912 | tf_op jit(solution)/shard_map/concatenate | solution.py:16
  36.2 0.8 slice_bitcast_fusion
  37.3 0.5 fusion.41
  37.7 0.5 fusion.65
  38.2 0.5 fusion.42
  38.7 0.5 fusion.43
  39.1 1.2 fusion.18
  40.3 1.8 fusion.59
  42.1 1.8 fusion.58
  43.9 1.8 fusion.57
  45.6 1.8 fusion.56
  47.5 1.2 fusion.17
  48.6 1.2 fusion.16
  49.8 1.2 fusion.15
  51.0 1.2 fusion.14
  52.2 2.2 fusion.3
  54.4 0.5 fusion.27
  54.8 0.7 fusion.129
  55.6 1.7 collective-permute-start.4
  57.3 0.3 collective-permute-start.5
  57.6 0.5 fusion.26
  58.1 0.5 fusion.25
  58.6 0.5 fusion.24
  59.1 0.5 fusion.23
  59.6 0.5 fusion.22
  60.1 0.5 fusion.21
  60.6 0.5 fusion.20
  61.2 0.5 fusion.19
  61.7 1.4 copy-done.4
  63.1 1.6 copy-done.2
  64.7 4.9 %fusion.12 = bf16[1,2,8,128,256]{4,3,2,1,0:T(8,128)(2,1)} fusion(f32[2,8,128,256]{3,2,1,0:T(8,128)S(1)} %copy-done.2, f32[2,8,128,256]{3,2,1,0:T(8,128)} %fusion.58, f32[2,8,128,256]{3,2,1,0:T(8,128)} %fusion.56, f32[2,8,128,256]{3,2,1,0:T(8,128)} %fusion.57, bf16[1,6,8,128,256]{4,3,2,1,0:T(8,128)(2,1)} %copy-done, bf16[5,256,256]{2,1,0:T(8,128)(2,1)} %param.7), kind=kOutput, calls=%fused_computation.31 | convolution fusion | flops 271056896 | bytes 10616832 | tf_op jit(solution)/shard_map/dot_general | solution.py:55
  69.6 0.5 fusion.74
  70.0 1.7 select_maximum_fusion
  71.7 0.5 fusion.32
  72.2 0.5 fusion.33
  72.7 0.5 fusion.34
  73.1 1.4 fusion.37
  74.5 0.5 fusion.35
  75.0 0.5 fusion.40
  75.5 0.5 fusion.28
  76.0 3.0 %fusion.13 = bf16[1,2,8,128,256]{4,3,2,1,0:T(8,128)(2,1)} fusion(f32[2,8,128,256]{3,2,1,0:T(8,128)S(1)} %fusion.28, f32[2,8,128,256]{3,2,1,0:T(8,128)S(1)} %fusion.32, f32[2,8,128,256]{3,2,1,0:T(8,128)S(1)} %fusion.33, f32[2,8,128,256]{3,2,1,0:T(8,128)S(1)} %fusion.74, f32[2,8,128,256]{3,2,1,0:T(8,128)S(1)} %fusion.34, f32[2,8,128,256]{3,2,1,0:T(8,128)S(1)} %fusion.35, ...), kind=kOutput, calls=%fused_computation.32 | convolution fusion | flops 273678336 | bytes 19136512 | tf_op jit(solution)/shard_map/dot_general | solution.py:40
  79.0 147.2 %all-reduce.5.cloned.1.call-done = (f32[3,3,256,256]{3,2,1,0:T(8,128)}, f32[5,256,256]{2,1,0:T(8,128)}) async-done(((f32[3,3,256,256]{3,2,1,0:T(8,128)}, f32[5,256,256]{2,1,0:T(8,128)}), (f32[3,3,256,256]{3,2,1,0:T(8,128)}, f32[5,256,256]{2,1,0:T(8,128)})) %all-reduce.5.cloned.1.call-update) | async-done | bytes 3670032 | tf_op jit(solution)/shard_map/psum | solution.py:99
  226.2 3.4 %broadcast_multiply_fusion = f32[3,3,256,256]{3,2,1,0:T(8,128)} fusion(f32[3,3,256,256]{3,2,1,0:T(8,128)} %get-tuple-element.4), kind=kLoop, calls=%fused_computation.33 | loop fusion | flops 589824 | bytes 4718592 | tf_op jit(solution)/shard_map/mul | solution.py:102
  229.5 1.2 broadcast_multiply_fusion.1
  (21 shorter events, 0.7 us)
Async XLA Ops:
  7.2 219.0 %all-reduce.5.cloned.1.call-start = ((), (), s32[]{:S(2)}) async-start(), calls=%async_computation | async-start | bytes 7340032 | tf_op jit(solution)/shard_map/psum | solution.py:99
  8.2 7.4 %collective-permute-start = (bf16[1,2,1,128,256]{4,3,2,1,0:T(8,128)(2,1)S(1)}, bf16[1,2,1,128,256]{4,3,2,1,0:T(8,128)(2,1)S(1)}, u32[]{:S(2)}, u32[]{:S(2)}) collective-permute-start(bf16[1,2,1,128,256]{4,3,2,1,0:T(8,128)(2,1)S(1)} %get-tuple-element.10), channel_id=1, source_target_pairs={{0,2},{2,0},{1,3},{3,1},{4,6},{6,4},{5,7},{7,5},{8,10},{10,8},{9,1... | collective-permute-start | bytes 393224 | tf_op jit(solution)/shard_map/ppermute | solution.py:14
  11.2 6.3 %copy-start.1 = (bf16[1,2,8,128,256]{4,3,2,1,0:T(8,128)(2,1)S(1)}, bf16[1,2,8,128,256]{4,3,2,1,0:T(8,128)(2,1)}, u32[]{:S(2)}) copy-start(bf16[1,2,8,128,256]{4,3,2,1,0:T(8,128)(2,1)} %param.4) | copy-start | bytes 3145732
  11.2 6.3 %collective-permute-start.1 = (bf16[1,2,1,128,256]{4,3,2,1,0:T(8,128)(2,1)S(1)}, bf16[1,2,1,128,256]{4,3,2,1,0:T(8,128)(2,1)S(1)}, u32[]{:S(2)}, u32[]{:S(2)}) collective-permute-start(bf16[1,2,1,128,256]{4,3,2,1,0:T(8,128)(2,1)S(1)} %get-tuple-element.11), channel_id=1, source_target_pairs={{2,0},{0,2},{3,1},{1,3},{6,4},{4,6},{7,5},{5,7},{10,8},{8,10},{11,... | collective-permute-start | bytes 393224 | tf_op jit(solution)/shard_map/ppermute | solution.py:15
  13.1 5.2 %copy-start.6 = (bf16[3,3,256,256]{3,2,1,0:T(8,128)(2,1)S(1)}, bf16[3,3,256,256]{3,2,1,0:T(8,128)(2,1)}, u32[]{:S(2)}) copy-start(bf16[3,3,256,256]{3,2,1,0:T(8,128)(2,1)} %param.6) | copy-start | bytes 3538948
  22.7 1.2 copy-start.3
  24.1 6.1 %collective-permute-start.3 = (bf16[2,1,2,8,128,256]{5,4,3,2,1,0:T(8,128)(2,1)S(1)}, bf16[2,1,2,8,128,256]{5,4,3,2,1,0:T(8,128)(2,1)S(1)}, u32[]{:S(2)}, u32[]{:S(2)}) collective-permute-start(bf16[2,1,2,8,128,256]{5,4,3,2,1,0:T(8,128)(2,1)S(1)} %pad_maximum_fusion.1), channel_id=1, source_target_pairs={{4,0},{8,4},{12,8},{16,12},{20,16},{24,20},{28,24},{5,1},{9,5},{13... | collective-permute-start | bytes 6291464 | tf_op jit(solution)/shard_map/ppermute | solution.py:15
  25.4 6.8 %collective-permute-start.2 = (bf16[2,1,2,8,128,256]{5,4,3,2,1,0:T(8,128)(2,1)S(1)}, bf16[2,1,2,8,128,256]{5,4,3,2,1,0:T(8,128)(2,1)S(1)}, u32[]{:S(2)}, u32[]{:S(2)}) collective-permute-start(bf16[2,1,2,8,128,256]{5,4,3,2,1,0:T(8,128)(2,1)S(1)} %pad_maximum_fusion.1), channel_id=1, source_target_pairs={{0,4},{4,8},{8,12},{12,16},{16,20},{20,24},{24,28},{1,5},{5,9},{9,... | collective-permute-start | bytes 6291464 | tf_op jit(solution)/shard_map/ppermute | solution.py:14
  36.2 1.1 copy-start.5
  37.0 14.0 %copy-start = (bf16[1,6,8,128,256]{4,3,2,1,0:T(8,128)(2,1)}, bf16[1,6,8,128,256]{4,3,2,1,0:T(8,128)(2,1)S(1)}, u32[]{:S(2)}) copy-start(bf16[1,6,8,128,256]{4,3,2,1,0:T(8,128)(2,1)S(1)} %get-tuple-element.7) | copy-start | bytes 9437188
  55.6 14.5 %collective-permute-start.4 = (bf16[1,2,1,128,256]{4,3,2,1,0:T(8,128)(2,1)}, bf16[1,2,1,128,256]{4,3,2,1,0:T(8,128)(2,1)}, u32[]{:S(2)}, u32[]{:S(2)}) collective-permute-start(bf16[1,2,1,128,256]{4,3,2,1,0:T(8,128)(2,1)} %get-tuple-element.8), channel_id=1, source_target_pairs={{0,2},{2,0},{1,3},{3,1},{4,6},{6,4},{5,7},{7,5},{8,10},{10,8},{9,1... | collective-permute-start | bytes 393224 | tf_op jit(solution)/shard_map/ppermute | solution.py:14
  57.3 12.7 %collective-permute-start.5 = (bf16[1,2,1,128,256]{4,3,2,1,0:T(8,128)(2,1)}, bf16[1,2,1,128,256]{4,3,2,1,0:T(8,128)(2,1)}, u32[]{:S(2)}, u32[]{:S(2)}) collective-permute-start(bf16[1,2,1,128,256]{4,3,2,1,0:T(8,128)(2,1)} %get-tuple-element.9), channel_id=1, source_target_pairs={{2,0},{0,2},{3,1},{1,3},{6,4},{4,6},{7,5},{5,7},{10,8},{8,10},{11,... | collective-permute-start | bytes 393224 | tf_op jit(solution)/shard_map/ppermute | solution.py:15
  61.7 1.4 copy-start.4
  63.1 1.6 copy-start.2
  64.7 4.9 %copy-start.7 = (bf16[3,3,256,256]{3,2,1,0:T(8,128)(2,1)S(1)}, bf16[3,3,256,256]{3,2,1,0:T(8,128)(2,1)}, u32[]{:S(2)}) copy-start(bf16[3,3,256,256]{3,2,1,0:T(8,128)(2,1)} %param.6) | copy-start | bytes 3538948
  226.2 3.4 %copy-start.8 = (f32[5,256,256]{2,1,0:T(8,128)S(1)}, f32[5,256,256]{2,1,0:T(8,128)}, u32[]{:S(2)}) copy-start(f32[5,256,256]{2,1,0:T(8,128)} %get-tuple-element.5) | copy-start | bytes 3932164
Sparse Core Ops, SparseCore 0:
  63.2 162.8 all-reduce.4
where the time goes:
time: 238 us
  waiting for transfers between devices  155 us (65%)
  matrix products  40.3 us (17%)
  between operations  14.3 us (6%)
  other arithmetic  11.7 us (5%)
  starting transfers between devices  9.82 us (4%)
  local copies, waits for them, and re-layouts  6.32 us (3%)
    psum x1, waiting for transfers between devices, shards(): lax.psum((spatial_sum, temporal_sum), ('tm', 'space', 'samples'))  147 us
    dot_general x18, matrix products, spatial_apply(): jnp.dot(piece, tap, preferred_element_type=jnp.float32).reshape(total.shape)  13.9 us
    dot_general x5, matrix products, temporal_apply(): jnp.dot(shifted, weight[k], preferred_element_type=jnp.float32)  12 us
    ppermute x3, starting transfers between devices, padded_2(): before = lax.ppermute(last, axis, up)  8.12 us
    concatenate x3, other arithmetic, padded_2(): shard = jnp.concatenate([before, shard, after], axis=dim)  6.28 us
    dot_general x5, matrix products, temporal_apply(): sums.append(jnp.dot(shifted.T, middle, preferred_element_type=jnp.float32))  5.87 us
  transfers between devices with their start and end apart: 7, of which 5 were waited for; matrix products, arithmetic and copies ran while one was open for 8% of the time, Pallas kernels for 0%

commit v1 on v0

v1 whole, which is shorter than its diff:
```python
import functools

import jax
import jax.numpy as jnp
from jax import lax
from jax.experimental import pallas as pl
from jax.experimental.pallas import tpu as pltpu
from jax.sharding import PartitionSpec as P

F32 = jnp.float32
BF16 = jnp.bfloat16
MESH = pl.DeviceIdType.MESH
ROOT = 0.7978845608028654
CUBE = 0.044715
ALIGN = 16


def dot(a, b):
    return jnp.dot(a, b, preferred_element_type=F32)


def bits_of(size):
    return [b for b in range(size.bit_length()) if (1 << b) < size]


def plan(streams, orders):
    offset, steps_of = 0, []
    for (base, rows), order in zip(streams, orders):
        steps, now = [], rows
        for axis, bit in order:
            halve = now % (2 * ALIGN) == 0 and now > 4 * ALIGN + ALIGN
            size = now // 2 if halve else now
            steps.append((axis, bit, halve, size, offset))
            offset += size
            now = size
        steps_of.append(steps)
    return steps_of, offset


def kernel(
    sizes, streams, steps_of,
    x_hbm, g_hbm, w_hbm, wt_hbm,
    block_ref, fg_ref, grads_ref,
    xc, xs, xt, xhalo, gbuf, abuf, at, deriv, hgc, hgs, hghalo,
    w, wback, wt, wtback, acc, gath, sbuf, rbuf,
    lsem, hsend, hrecv, fsend, frecv, rsend, rrecv, asend, arecv,
):
    frames, height, wide, chans = xc.shape
    me, sp = lax.axis_index("tm"), lax.axis_index("space")
    here = {name: lax.axis_index(name) for name in sizes}
    has_prev, has_next = me > 0, me < sizes["tm"] - 1
    below = {"tm": lax.rem(me + sizes["tm"] - 1, sizes["tm"])}
    above = {"tm": lax.rem(me + 1, sizes["tm"])}
    left = {"space": lax.rem(sp + sizes["space"] - 1, sizes["space"])}
    right = {"space": lax.rem(sp + 1, sizes["space"])}

    def partner(axis, bit):
        at_bit = lax.rem(here[axis] // (1 << bit), 2)
        return {axis: here[axis] + (1 - 2 * at_bit) * (1 << bit)}, at_bit

    local = [
        pltpu.make_async_copy(src, dst, lsem.at[n])
        for n, (src, dst) in enumerate(
            ((x_hbm, xc), (w_hbm, w), (wt_hbm, wt), (g_hbm, gbuf.at[pl.ds(2, frames)]))
        )
    ]
    for copy in local:
        copy.start()

    barrier = pltpu.get_barrier_semaphore()
    peers = [left, right] + [partner(a, b)[0] for a in sizes for b in bits_of(sizes[a])]
    for peer in peers:
        pl.semaphore_signal(barrier, inc=1, device_id=peer, device_id_type=MESH)

    @pl.when(has_prev)
    def _():
        pl.semaphore_signal(barrier, inc=1, device_id=below, device_id_type=MESH)

    @pl.when(has_next)
    def _():
        pl.semaphore_signal(barrier, inc=1, device_id=above, device_id_type=MESH)

    pl.semaphore_wait(
        barrier, len(peers) + jnp.minimum(me, 1) + jnp.minimum(sizes["tm"] - 1 - me, 1)
    )

    def remote(src, dst, send, recv, peer):
        return pltpu.make_async_remote_copy(
            src_ref=src, dst_ref=dst, send_sem=send, recv_sem=recv,
            device_id=peer, device_id_type=MESH,
        )

    def row_pair(src, halo, send, recv, first):
        return [
            remote(src.at[:, height - 1], halo.at[0], send.at[first], recv.at[first], right),
            remote(src.at[:, 0], halo.at[1], send.at[first + 1], recv.at[first + 1], left),
        ]

    def frame_pair(src, start, buf, first):
        return (
            remote(
                src.at[pl.ds(start + frames - 2, 2)], buf.at[pl.ds(0, 2)],
                fsend.at[first], frecv.at[first], above,
            ),
            remote(
                src.at[pl.ds(start, 2)], buf.at[pl.ds(2 + frames, 2)],
                fsend.at[first + 1], frecv.at[first + 1], below,
            ),
        )

    def frames_start(pair):
        @pl.when(has_next)
        def _():
            pair[0].start()

        @pl.when(has_prev)
        def _():
            pair[1].start()

    def frames_wait(pair):
        @pl.when(has_next)
        def _():
            pair[0].wait_send()
            pair[1].wait_recv()

        @pl.when(has_prev)
        def _():
            pair[1].wait_send()
            pair[0].wait_recv()

    x_rows = row_pair(x_hbm, xhalo, hsend, hrecv, 0)
    g_frames = frame_pair(g_hbm, 0, gbuf, 0)
    frames_start(g_frames)
    for copy in x_rows:
        copy.start()

    for buf in (gbuf, abuf):
        @pl.when(jnp.logical_not(has_prev))
        def _(buf=buf):
            buf[0:2] = jnp.zeros((2, height, wide, chans), BF16)

        @pl.when(jnp.logical_not(has_next))
        def _(buf=buf):
            buf[2 + frames :] = jnp.zeros((2, height, wide, chans), BF16)

    cell = lax.broadcasted_iota(jnp.int32, (wide, chans), 0)

    def spread(value, dst, f, r):
        full = value.astype(F32)
        lo = jnp.where(cell == 0, 0.0, pltpu.roll(full, 1, 0)).astype(BF16)
        hi = jnp.where(cell == wide - 1, 0.0, pltpu.roll(full, wide - 1, 0)).astype(BF16)
        dst[f, r, :, 0:chans] = lo
        dst[f, r, :, chans : 2 * chans] = value
        dst[f, r, :, 2 * chans : 3 * chans] = hi

    local[0].wait()

    @pl.loop(0, frames * height)
    def _(n):
        f, r = n // height, lax.rem(n, height)
        value = xc[f, r]
        spread(value, xs, f, r + 1)
        xt[f, r + 1] = value.T

    local[1].wait()

    def settle(hidden, f, r, rows):
        square = hidden * hidden
        t = jnp.tanh(ROOT * hidden * (1.0 + CUBE * square))
        half = 0.5 * (1.0 + t)
        act = (hidden * half).astype(BF16)
        slope = half + (0.5 * ROOT) * hidden * (1.0 - t * t) * (1.0 + (3.0 * CUBE) * square)
        deriv[f, pl.ds(r, rows)] = slope.reshape(rows, wide, chans)
        abuf[2 + f, pl.ds(r, rows)] = act.reshape(rows, wide, chans)
        for n in range(rows):
            at[f, r + n] = act[n * wide : (n + 1) * wide].T

    def taps(src, f, r, rows):
        return jnp.concatenate(
            [src[f, pl.ds(r + i, rows)].reshape(rows * wide, 3 * chans) for i in range(3)], axis=1
        )

    @pl.loop(0, frames)
    def _(f):
        settle(dot(taps(xs, f, 1, height - 2), w[...]), f, 1, height - 2)

    for n in range(9):
        wback[(8 - n) * chans : (9 - n) * chans] = w[n * chans : (n + 1) * chans].T
    local[2].wait()
    for n in range(5):
        wtback[(4 - n) * chans : (5 - n) * chans] = wt[n * chans : (n + 1) * chans].T

    for copy in x_rows:
        copy.wait()

    @pl.loop(0, frames)
    def _(f):
        for side in range(2):
            value = xhalo[side, f]
            spread(value, xs, f, side * (height + 1))
            xt[f, side * (height + 1)] = value.T

    @pl.loop(0, frames)
    def _(f):
        lhs = jnp.concatenate([taps(xs, f, 0, 1), taps(xs, f, height - 1, 1)], axis=0)
        hidden = dot(lhs, w[...])
        settle(hidden[:wide], f, 0, 1)
        settle(hidden[wide:], f, height - 1, 1)

    a_frames = frame_pair(abuf, 2, abuf, 2)
    frames_start(a_frames)

    local[3].wait()
    frames_wait(g_frames)

    def over_frames(buf, f, weight):
        lhs = jnp.concatenate(
            [buf[f + k].reshape(height * wide, chans) for k in range(5)], axis=1
        )
        return dot(lhs, weight[...])

    @pl.loop(0, frames)
    def _(f):
        act_grad = over_frames(gbuf, f, wtback).astype(BF16).astype(F32)
        hg = act_grad * deriv[f].reshape(height * wide, chans)
        hgc[f] = hg.astype(BF16).reshape(height, wide, chans)

    h_rows = row_pair(hgc, hghalo, hsend, hrecv, 2)
    for copy in h_rows:
        copy.start()

    def exchange(stream, k):
        axis, bit, halve, size, offset = steps_of[stream][k]
        peer, at_bit = partner(axis, bit)
        start = segment(stream, k)
        source = start + (1 - at_bit) * size if halve else start
        copy = remote(
            sbuf.at[pl.ds(offset, size)], rbuf.at[pl.ds(offset, size)],
            rsend.at[stream, k], rrecv.at[stream, k], peer,
        )
        return copy, pl.multiple_of(source, ALIGN), size, offset

    def segment(stream, k):
        start = streams[stream][0]
        for axis, bit, halve, size, _ in steps_of[stream][:k]:
            if halve:
                start = start + partner(axis, bit)[1] * size
        return pl.multiple_of(start, ALIGN) if k else start

    def reduce_start(stream, k):
        copy, source, size, offset = exchange(stream, k)
        sbuf[offset : offset + size] = acc[pl.ds(source, size)].astype(BF16)
        copy.start()

    def reduce_finish(stream, k):
        copy, _, size, offset = exchange(stream, k)
        copy.wait()
        halve = steps_of[stream][k][2]
        keep = segment(stream, k + 1)
        got = rbuf[offset : offset + size].astype(F32)
        if halve:
            mine = acc[pl.ds(keep, size)]
        else:
            mine = sbuf[offset : offset + size].astype(F32)
        acc[pl.ds(keep, size)] = mine + got

    def round_sum(stream):
        size = steps_of[stream][-1][3]
        place = segment(stream, len(steps_of[stream]))
        gath[pl.ds(place, size)] = acc[pl.ds(place, size)].astype(BF16)

    def gather_copy(stream, k):
        axis, bit, _, size, _ = steps_of[stream][k]
        place = gath.at[pl.ds(segment(stream, k + 1), size)]
        return remote(
            place, place, asend.at[stream, k], arecv.at[stream, k], partner(axis, bit)[0]
        )

    def states(stream):
        count = len(steps_of[stream])
        halving = [k for k in range(count) if steps_of[stream][k][2]][::-1]
        moves = [lambda: reduce_start(stream, 0)]
        for k in range(1, count):
            def move(k=k):
                reduce_finish(stream, k - 1)
                reduce_start(stream, k)
            moves.append(move)

        def turn():
            reduce_finish(stream, count - 1)
            round_sum(stream)
            gather_copy(stream, halving[0]).start()

        moves.append(turn)
        for last, now in zip(halving, halving[1:]):
            def move(last=last, now=now):
                gather_copy(stream, last).wait()
                gather_copy(stream, now).start()
            moves.append(move)
        moves.append(lambda: gather_copy(stream, halving[-1]).wait())
        return moves

    queues = [states(s) for s in range(len(streams))]

    def advance(*which):
        for s in which:
            if queues[s]:
                queues[s].pop(0)()

    turned = jnp.concatenate(
        [at[f, r] for f in range(frames) for r in range(height)], axis=1
    )
    for k in range(5):
        rhs = gbuf[4 - k : 4 - k + frames].reshape(frames * height * wide, chans)
        acc[k * chans : (k + 1) * chans] = dot(turned, rhs)
    advance(0)

    @pl.loop(0, frames * height)
    def _(n):
        f, r = n // height, lax.rem(n, height)
        spread(hgc[f, r], hgs, f, r + 1)

    for i in range(3):
        lhs = jnp.concatenate(
            [xt[f, r + i] for f in range(frames) for r in range(height)], axis=1
        )
        rhs = hgs[:, 1 : height + 1].reshape(frames * height * wide, 3 * chans)
        out = dot(lhs, rhs)
        for j in range(3):
            first = (5 + 3 * i + j) * chans
            acc[first : first + chans] = out[:, (2 - j) * chans : (3 - j) * chans]
        if i == 0:
            advance(0)
        if i == 1:
            advance(1)
    advance(2, 0)

    for copy in h_rows:
        copy.wait()

    @pl.loop(0, frames)
    def _(f):
        for side in range(2):
            spread(hghalo[side, f], hgs, f, side * (height + 1))

    advance(1, 2, 0)
    for f in range(frames):
        fg_ref[f] = (
            dot(taps(hgs, f, 0, height), wback[...]).astype(BF16).reshape(height, wide, chans)
        )
        advance(1, 2, 0)

    frames_wait(a_frames)
    for f in range(frames):
        block_ref[f] = over_frames(abuf, f, wt).astype(BF16).reshape(height, wide, chans)
        advance(1, 2, 0)
    while any(queues):
        advance(1, 2, 0)
    grads_ref[...] = gath[...]


def shards(sizes, fields, out_grad, spatial_weight, temporal_weight):
    samples, frames, height, wide, chans = fields.shape
    ntaps, ktaps = 9, temporal_weight.shape[0]
    streams = [
        (0, ktaps * chans),
        (ktaps * chans, 5 * chans),
        ((ktaps + 5) * chans, 4 * chans),
    ]
    core = [("tm", 0)]
    chips = [("tm", b) for b in bits_of(sizes["tm"])[1:]]
    space = [("space", b) for b in bits_of(sizes["space"])]
    samp = [("samples", b) for b in bits_of(sizes["samples"])]
    orders = [
        core + samp + space + chips,
        core + space + samp + chips,
        core + samp + space + chips,
    ]
    steps_of, buffer_rows = plan(streams, orders)
    most = max(len(steps) for steps in steps_of)
    rows_all = (ntaps + ktaps) * chans
    tile = (height, wide, chans)
    sem = pltpu.SemaphoreType.DMA
    any_spec = pl.BlockSpec(memory_space=pl.ANY)
    vmem_spec = pl.BlockSpec(memory_space=pltpu.VMEM)
    block, fg, grads = pl.pallas_call(
        functools.partial(kernel, sizes, streams, steps_of),
        out_shape=(
            jax.ShapeDtypeStruct((samples * frames,) + tile, BF16),
            jax.ShapeDtypeStruct((samples * frames,) + tile, BF16),
            jax.ShapeDtypeStruct((rows_all, chans), BF16),
        ),
        in_specs=[any_spec] * 4,
        out_specs=(vmem_spec, vmem_spec, vmem_spec),
        scratch_shapes=[
            pltpu.VMEM((frames,) + tile, BF16),
            pltpu.VMEM((frames, height + 2, wide, 3 * chans), BF16),
            pltpu.VMEM((frames, height + 2, chans, wide), BF16),
            pltpu.VMEM((2, frames, wide, chans), BF16),
            pltpu.VMEM((frames + 4,) + tile, BF16),
            pltpu.VMEM((frames + 4,) + tile, BF16),
            pltpu.VMEM((frames, height, chans, wide), BF16),
            pltpu.VMEM((frames,) + tile, F32),
            pltpu.VMEM((frames,) + tile, BF16),
            pltpu.VMEM((frames, height + 2, wide, 3 * chans), BF16),
            pltpu.VMEM((2, frames, wide, chans), BF16),
            pltpu.VMEM((ntaps * chans, chans), BF16),
            pltpu.VMEM((ntaps * chans, chans), BF16),
            pltpu.VMEM((ktaps * chans, chans), BF16),
            pltpu.VMEM((ktaps * chans, chans), BF16),
            pltpu.VMEM((rows_all, chans), F32),
            pltpu.VMEM((rows_all, chans), BF16),
            pltpu.VMEM((buffer_rows, chans), BF16),
            pltpu.VMEM((buffer_rows, chans), BF16),
            sem((4,)), sem((4,)), sem((4,)), sem((4,)), sem((4,)),
            sem((3, most)), sem((3, most)), sem((3, most)), sem((3, most)),
        ],
        compiler_params=pltpu.CompilerParams(
            collective_id=0, has_side_effects=True, vmem_limit_bytes=60 * 1024 * 1024
        ),
    )(
        fields.reshape((samples * frames,) + tile),
        out_grad.reshape((samples * frames,) + tile),
        spatial_weight.reshape(ntaps * chans, chans),
        temporal_weight.reshape(ktaps * chans, chans),
    )
    devices = sizes["tm"] * sizes["space"] * sizes["samples"]
    factor = (samples * frames * height * wide * devices) ** (-0.5)
    scaled = grads.astype(F32) * factor
    return (
        block.reshape(fields.shape),
        fg.reshape(fields.shape),
        scaled[ktaps * chans :].reshape(spatial_weight.shape),
        scaled[: ktaps * chans].reshape(temporal_weight.shape),
    )


def solution(mesh):
    split = P("samples", "tm", "space", None, None)
    return jax.shard_map(
        functools.partial(shards, dict(mesh.shape)),
        mesh=mesh,
        in_specs=(split, split, P(), P()),
        out_specs=(split, split, P(), P()),
        check_vma=False,
    )
```

time: 238 us -> 71.4 us (0.30)
  waiting for transfers between devices: 155 us -> 0 us
  Pallas kernels: 0 us -> 64.1 us
  matrix products: 40.3 us -> 0 us
  between operations: 14.3 us -> 0.65 us
  other arithmetic: 11.7 us -> 1.74 us
  starting transfers between devices: 9.82 us -> 0 us
    psum x1 -> x0, waiting for transfers between devices: 147 us -> none  [shards(): lax.psum((spatial_sum, temporal_sum), ('tm', 'space', 'samples'))]
    pallas_call x0 -> x1, Pallas kernels: none -> 64.1 us  [shards(): pl.pallas_call(functools.partial(kernel, sizes, streams, steps_of), out_s...]
    dot_general x42 -> x0, matrix products: 40.3 us -> none  [the longest x18 13.9 us: spatial_apply(): jnp.dot(piece, tap, preferred_element_type=jnp.float32).reshape(total.shape)]
    ppermute x6 -> x0, starting transfers between devices: 9.78 us -> none  [the longest x3 8.12 us: padded_2(): before = lax.ppermute(last, axis, up)]
    ppermute x6 -> x0, waiting for transfers between devices: 7.93 us -> none  [the longest x3 4.57 us: padded_2(): before = lax.ppermute(last, axis, up)]
    concatenate x3 -> x0, other arithmetic: 6.28 us -> none  [padded_2(): shard = jnp.concatenate([before, shard, after], axis=dim)]
    mul x2 -> x1, other arithmetic: 4.53 us -> 1.74 us  [shards(): scaled = grads.astype(F32) * factor]
  transfers between devices with their start and end apart: 7 -> 0, of which waited for: 5 -> 0; matrix products, arithmetic and copies ran while one was open for 8% -> 0% of each run, Pallas kernels for 0% -> 0%
where the time goes in v1:
time: 71.4 us; the launch traced here: 71.2 us
  Pallas kernels  64.1 us (90%)
  local copies, waits for them, and re-layouts  4.66 us (7%)
  other arithmetic  1.74 us (2%)
    pallas_call x1, Pallas kernels, shards(): pl.pallas_call(functools.partial(kernel, sizes, streams, steps_of), out_s...  64.1 us
    unnamed x6, local copies, waits for them, and re-layouts  1.96 us
    mul x1, other arithmetic, shards(): scaled = grads.astype(F32) * factor  1.74 us
    slice x1, local copies, waits for them, and re-layouts, shards(): scaled[ktaps * chans:].reshape(spatial_weight.shape)  1.56 us

profile of v1, /device:TPU:0, one launch (start us, length us, event | category | flops | bytes accessed | tf_op | source)
XLA Modules:
  0.0 71.2 jit_solution(15266219651858554341)
XLA Ops:
  0.6 64.1 %shard_map.75 = (bf16[2,8,128,256]{3,2,1,0:T(8,128)(2,1)}, bf16[2,8,128,256]{3,2,1,0:T(8,128)(2,1)}, bf16[3584,256]{1,0:T(8,128)(2,1)}) custom-call(bf16[2,8,128,256]{3,2,1,0:T(8,128)(2,1)} %bitcast.13, bf16[2,8,128,256]{3,2,1,0:T(8,128)(2,1)} %bitcast.14, bf16[2304,256]{1,0:T(8,128)(2,1)} %bitcast.10, bf16[1280,256]{1,0:T(8,128)(2,1)} %bitcast.15), custom_call_target="tpu_custom_call" | custom-call | tf_op jit(solution)/shard_map/pallas_call | solution.py:386
  64.8 1.7 %convert_multiply_fusion = f32[3584,256]{1,0:T(8,128)S(1)} fusion(bf16[3584,256]{1,0:T(8,128)(2,1)} %get-tuple-element.9), kind=kLoop, calls=%fused_computation | loop fusion | flops 1835008 | bytes 5505024 | tf_op jit(solution)/shard_map/mul | solution.py:429
  66.5 1.1 %slice.9 = f32[1280,256]{1,0:T(8,128)} slice(f32[3584,256]{1,0:T(8,128)S(1)} %convert_multiply_fusion), slice={[0:1280], [0:256]} | slice | bytes 2621440 | tf_op jit(solution)/shard_map/slice | solution.py:434
  67.7 0.0 copy-start.1
  67.7 0.0 copy-start
  67.7 1.6 %slice.8 = f32[2304,256]{1,0:T(8,128)} slice(f32[3584,256]{1,0:T(8,128)S(1)} %convert_multiply_fusion), slice={[1280:3584], [0:256]} | slice | bytes 4718592 | tf_op jit(solution)/shard_map/slice | solution.py:433
  69.2 0.0 copy-done.1
  69.2 1.0 %copy.10 = bf16[1,2,8,128,256]{4,3,2,1,0:T(8,128)(2,1)} copy(bf16[1,2,8,128,256]{4,3,2,1,0:T(8,128)(2,1)S(1)} %bitcast.12) | data formatting | bytes 2097152
  70.2 0.0 copy-done
  70.2 1.0 %copy.11 = bf16[1,2,8,128,256]{4,3,2,1,0:T(8,128)(2,1)} copy(bf16[1,2,8,128,256]{4,3,2,1,0:T(8,128)(2,1)S(1)} %bitcast.11) | data formatting | bytes 2097152
Async XLA Ops:
  67.7 1.6 %copy-start.1 = (bf16[2,8,128,256]{3,2,1,0:T(8,128)(2,1)S(1)}, bf16[2,8,128,256]{3,2,1,0:T(8,128)(2,1)}, u32[]{:S(2)}) copy-start(bf16[2,8,128,256]{3,2,1,0:T(8,128)(2,1)} %get-tuple-element.7) | copy-start | bytes 3145732
  67.7 2.6 %copy-start = (bf16[2,8,128,256]{3,2,1,0:T(8,128)(2,1)S(1)}, bf16[2,8,128,256]{3,2,1,0:T(8,128)(2,1)}, u32[]{:S(2)}) copy-start(bf16[2,8,128,256]{3,2,1,0:T(8,128)(2,1)} %get-tuple-element.8) | copy-start | bytes 3145732

commit v2 on v1

--- a/solution.py
+++ b/solution.py
@@ -23,27 +23,35 @@
     return [b for b in range(size.bit_length()) if (1 << b) < size]
 
 
-def plan(streams, orders):
+def plan(streams, orders, group):
     offset, steps_of = 0, []
-    for (base, rows), order in zip(streams, orders):
+    for (_, rows), order in zip(streams, orders):
         steps, now = [], rows
         for axis, bit in order:
-            halve = now % (2 * ALIGN) == 0 and now > 4 * ALIGN + ALIGN
-            size = now // 2 if halve else now
-            steps.append((axis, bit, halve, size, offset))
-            offset += size
-            now = size
+            halve = now % (2 * ALIGN) == 0
+            now = now // 2 if halve else now
+            steps.append(("halve" if halve else "whole", axis, bit, now, offset))
+            offset += now
+        axis, shift, size = group
+        if size > 1 and now % (size * ALIGN) == 0:
+            now //= size
+            steps.append(("group", axis, shift, now, offset))
+            offset += now * (size - 1)
+        elif size > 1:
+            for bit in bits_of(size):
+                steps.append(("whole", axis, bit + shift, now, offset))
+                offset += now
         steps_of.append(steps)
     return steps_of, offset
 
 
 def kernel(
-    sizes, streams, steps_of,
+    sizes, streams, steps_of, chips,
     x_hbm, g_hbm, w_hbm, wt_hbm,
-    block_ref, fg_ref, grads_ref,
+    block_ref, fg_ref, sgrad_ref, tgrad_ref,
     xc, xs, xt, xhalo, gbuf, abuf, at, deriv, hgc, hgs, hghalo,
     w, wback, wt, wtback, acc, gath, sbuf, rbuf,
-    lsem, hsend, hrecv, fsend, frecv, rsend, rrecv, asend, arecv,
+    stage, lsem, osem, hsend, hrecv, fsend, frecv, rsend, rrecv, asend, arecv,
 ):
     frames, height, wide, chans = xc.shape
     me, sp = lax.axis_index("tm"), lax.axis_index("space")
@@ -67,8 +75,14 @@
     for copy in local:
         copy.start()
 
+    chip, core = here["tm"] // 2, lax.rem(here["tm"], 2)
+
+    def chip_peer(step):
+        return {"tm": lax.rem(chip + step + chips, chips) * 2 + core}
+
     barrier = pltpu.get_barrier_semaphore()
-    peers = [left, right] + [partner(a, b)[0] for a in sizes for b in bits_of(sizes[a])]
+    peers = [left, right, partner("tm", 0)[0]] + [chip_peer(d) for d in range(1, chips)]
+    peers += [partner(a, b)[0] for a in ("space", "samples") for b in bits_of(sizes[a])]
     for peer in peers:
         pl.semaphore_signal(barrier, inc=1, device_id=peer, device_id_type=MESH)
 
@@ -210,75 +224,99 @@
     a_frames = frame_pair(abuf, 2, abuf, 2)
     frames_start(a_frames)
 
-    local[3].wait()
-    frames_wait(g_frames)
-
-    def over_frames(buf, f, weight):
-        lhs = jnp.concatenate(
-            [buf[f + k].reshape(height * wide, chans) for k in range(5)], axis=1
-        )
-        return dot(lhs, weight[...])
-
-    @pl.loop(0, frames)
-    def _(f):
-        act_grad = over_frames(gbuf, f, wtback).astype(BF16).astype(F32)
-        hg = act_grad * deriv[f].reshape(height * wide, chans)
-        hgc[f] = hg.astype(BF16).reshape(height, wide, chans)
-
-    h_rows = row_pair(hgc, hghalo, hsend, hrecv, 2)
-    for copy in h_rows:
-        copy.start()
-
-    def exchange(stream, k):
-        axis, bit, halve, size, offset = steps_of[stream][k]
-        peer, at_bit = partner(axis, bit)
-        start = segment(stream, k)
-        source = start + (1 - at_bit) * size if halve else start
-        copy = remote(
-            sbuf.at[pl.ds(offset, size)], rbuf.at[pl.ds(offset, size)],
-            rsend.at[stream, k], rrecv.at[stream, k], peer,
-        )
-        return copy, pl.multiple_of(source, ALIGN), size, offset
-
     def segment(stream, k):
         start = streams[stream][0]
-        for axis, bit, halve, size, _ in steps_of[stream][:k]:
-            if halve:
+        for kind, axis, bit, size, _ in steps_of[stream][:k]:
+            if kind == "halve":
                 start = start + partner(axis, bit)[1] * size
+            if kind == "group":
+                start = start + chip * size
         return pl.multiple_of(start, ALIGN) if k else start
 
+    def reduce_copies(stream, k):
+        kind, axis, bit, size, offset = steps_of[stream][k]
+        start = segment(stream, k)
+        if kind == "group":
+            moves = [
+                (chip_peer(d), start + lax.rem(chip + d, chips) * size) for d in range(1, chips)
+            ]
+        else:
+            peer, at_bit = partner(axis, bit)
+            moves = [(peer, start + (1 - at_bit) * size if kind == "halve" else start)]
+        out = []
+        for n, (peer, source) in enumerate(moves):
+            place = pl.ds(offset + n * size, size)
+            out.append(
+                (
+                    remote(
+                        sbuf.at[place], rbuf.at[place],
+                        rsend.at[stream, k + n], rrecv.at[stream, k + n], peer,
+                    ),
+                    place,
+                    pl.ds(pl.multiple_of(source, ALIGN), size),
+                )
+            )
+        return out
+
     def reduce_start(stream, k):
-        copy, source, size, offset = exchange(stream, k)
-        sbuf[offset : offset + size] = acc[pl.ds(source, size)].astype(BF16)
-        copy.start()
+        for copy, place, source in reduce_copies(stream, k):
+            sbuf[place] = acc[source].astype(BF16)
+            copy.start()
 
     def reduce_finish(stream, k):
-        copy, _, size, offset = exchange(stream, k)
-        copy.wait()
-        halve = steps_of[stream][k][2]
-        keep = segment(stream, k + 1)
-        got = rbuf[offset : offset + size].astype(F32)
-        if halve:
-            mine = acc[pl.ds(keep, size)]
+        copies = reduce_copies(stream, k)
+        for copy, _, _ in copies:
+            copy.wait()
+        kind, _, _, size, _ = steps_of[stream][k]
+        keep = pl.ds(segment(stream, k + 1), size)
+        total = sbuf[copies[0][1]].astype(F32) if kind == "whole" else acc[keep]
+        for _, place, _ in copies:
+            total = total + rbuf[place].astype(F32)
+        acc[keep] = total
+
+    def gather_copies(stream, k):
+        kind, axis, bit, size, _ = steps_of[stream][k]
+        place = gath.at[pl.ds(segment(stream, k + 1), size)]
+        if kind == "group":
+            to = [chip_peer(d) for d in range(1, chips)]
         else:
-            mine = sbuf[offset : offset + size].astype(F32)
-        acc[pl.ds(keep, size)] = mine + got
-
-    def round_sum(stream):
-        size = steps_of[stream][-1][3]
-        place = segment(stream, len(steps_of[stream]))
-        gath[pl.ds(place, size)] = acc[pl.ds(place, size)].astype(BF16)
-
-    def gather_copy(stream, k):
-        axis, bit, _, size, _ = steps_of[stream][k]
-        place = gath.at[pl.ds(segment(stream, k + 1), size)]
-        return remote(
-            place, place, asend.at[stream, k], arecv.at[stream, k], partner(axis, bit)[0]
-        )
+            to = [partner(axis, bit)[0]]
+        return [
+            remote(place, place, asend.at[stream, k + n], arecv.at[stream, k + n], peer)
+            for n, peer in enumerate(to)
+        ]
+
+    def gather_start(stream, k):
+        for copy in gather_copies(stream, k):
+            copy.start()
+
+    def gather_finish(stream, k):
+        for copy in gather_copies(stream, k):
+            copy.wait()
+
+    def out_copies(stream):
+        base, rows = streams[stream]
+        edge = 5 * chans
+        out = []
+        for n, (lo, hi, ref) in enumerate(
+            (
+                (base, min(base + rows, edge), tgrad_ref),
+                (max(base, edge), base + rows, sgrad_ref),
+            )
+        ):
+            if lo < hi:
+                out.append(
+                    pltpu.make_async_copy(
+                        gath.at[pl.ds(lo, hi - lo)],
+                        ref.at[pl.ds(lo - n * edge, hi - lo)],
+                        osem.at[2 * stream + n],
+                    )
+                )
+        return out
 
     def states(stream):
         count = len(steps_of[stream])
-        halving = [k for k in range(count) if steps_of[stream][k][2]][::-1]
+        back = [k for k in range(count) if steps_of[stream][k][0] != "whole"][::-1]
         moves = [lambda: reduce_start(stream, 0)]
         for k in range(1, count):
             def move(k=k):
@@ -288,16 +326,23 @@
 
         def turn():
             reduce_finish(stream, count - 1)
-            round_sum(stream)
-            gather_copy(stream, halving[0]).start()
+            place = pl.ds(segment(stream, count), steps_of[stream][-1][3])
+            gath[place] = acc[place].astype(BF16)
+            gather_start(stream, back[0])
 
         moves.append(turn)
-        for last, now in zip(halving, halving[1:]):
+        for last, now in zip(back, back[1:]):
             def move(last=last, now=now):
-                gather_copy(stream, last).wait()
-                gather_copy(stream, now).start()
+                gather_finish(stream, last)
+                gather_start(stream, now)
             moves.append(move)
-        moves.append(lambda: gather_copy(stream, halving[-1]).wait())
+
+        def close():
+            gather_finish(stream, back[-1])
+            for copy in out_copies(stream):
+                copy.start()
+
+        moves.append(close)
         return moves
 
     queues = [states(s) for s in range(len(streams))]
@@ -307,19 +352,51 @@
             if queues[s]:
                 queues[s].pop(0)()
 
-    turned = jnp.concatenate(
-        [at[f, r] for f in range(frames) for r in range(height)], axis=1
-    )
-    for k in range(5):
-        rhs = gbuf[4 - k : 4 - k + frames].reshape(frames * height * wide, chans)
-        acc[k * chans : (k + 1) * chans] = dot(turned, rhs)
-    advance(0)
+    def act_by_grad(k, first, last):
+        lhs = jnp.concatenate([at[u, r] for u in range(first, last) for r in range(height)], axis=1)
+        rhs = gbuf[4 - k + first : 4 - k + last]
+        return dot(lhs, rhs.reshape((last - first) * height * wide, chans))
+
+    local[3].wait()
+    own = [(max(0, k - 2), min(frames, frames + k - 2)) for k in range(5)]
+    for k, (first, last) in enumerate(own):
+        if first < last:
+            acc[k * chans : (k + 1) * chans] = act_by_grad(k, first, last)
+    frames_wait(g_frames)
+    for k, (first, last) in enumerate(own):
+        rows = slice(k * chans, (k + 1) * chans)
+        if first >= last:
+            acc[rows] = act_by_grad(k, 0, frames)
+        elif first > 0:
+            acc[rows] += act_by_grad(k, 0, first)
+        elif last < frames:
+            acc[rows] += act_by_grad(k, last, frames)
+        if k % 2:
+            advance(k // 2)
+
+    def over_frames(buf, f, weight):
+        lhs = jnp.concatenate(
+            [buf[f + k].reshape(height * wide, chans) for k in range(5)], axis=1
+        )
+        return dot(lhs, weight[...])
+
+    @pl.loop(0, frames)
+    def _(f):
+        act_grad = over_frames(gbuf, f, wtback).astype(BF16).astype(F32)
+        hg = act_grad * deriv[f].reshape(height * wide, chans)
+        hgc[f] = hg.astype(BF16).reshape(height, wide, chans)
+
+    h_rows = row_pair(hgc, hghalo, hsend, hrecv, 2)
+    for copy in h_rows:
+        copy.start()
+    advance(0, 1)
 
     @pl.loop(0, frames * height)
     def _(n):
         f, r = n // height, lax.rem(n, height)
         spread(hgc[f, r], hgs, f, r + 1)
 
+    ready = [(2, 3), (4,), (5, 6)]
     for i in range(3):
         lhs = jnp.concatenate(
             [xt[f, r + i] for f in range(frames) for r in range(height)], axis=1
@@ -329,11 +406,11 @@
         for j in range(3):
             first = (5 + 3 * i + j) * chans
             acc[first : first + chans] = out[:, (2 - j) * chans : (3 - j) * chans]
-        if i == 0:
-            advance(0)
-        if i == 1:
-            advance(1)
-    advance(2, 0)
+        advance(*ready[i])
+        if i:
+            advance(0, 1)
+        if i == 2:
+            advance(2, 3, 4)
 
     for copy in h_rows:
         copy.wait()
@@ -343,55 +420,66 @@
         for side in range(2):
             spread(hghalo[side, f], hgs, f, side * (height + 1))
 
-    advance(1, 2, 0)
+    def round_of_moves():
+        advance(*range(len(queues)))
+
+    done = []
+
+    def put(slot, value, out, f, r, rows):
+        stage[slot, f, r : r + rows] = value.astype(BF16).reshape(rows, wide, chans)
+        copy = pltpu.make_async_copy(
+            stage.at[slot, f, pl.ds(r, rows)],
+            out.at[f, pl.ds(r, rows)],
+            osem.at[2 * len(queues) + len(done)],
+        )
+        copy.start()
+        done.append(copy)
+
+    part = height // 2
+    round_of_moves()
     for f in range(frames):
-        fg_ref[f] = (
-            dot(taps(hgs, f, 0, height), wback[...]).astype(BF16).reshape(height, wide, chans)
-        )
-        advance(1, 2, 0)
+        for r in range(0, height, part):
+            put(0, dot(taps(hgs, f, r, part), wback[...]), fg_ref, f, r, part)
+            round_of_moves()
 
     frames_wait(a_frames)
     for f in range(frames):
-        block_ref[f] = over_frames(abuf, f, wt).astype(BF16).reshape(height, wide, chans)
-        advance(1, 2, 0)
+        put(1, over_frames(abuf, f, wt), block_ref, f, 0, height)
+        round_of_moves()
     while any(queues):
-        advance(1, 2, 0)
-    grads_ref[...] = gath[...]
+        round_of_moves()
+    for stream in range(len(queues)):
+        done.extend(out_copies(stream))
+    for copy in done:
+        copy.wait()
 
 
 def shards(sizes, fields, out_grad, spatial_weight, temporal_weight):
     samples, frames, height, wide, chans = fields.shape
     ntaps, ktaps = 9, temporal_weight.shape[0]
-    streams = [
-        (0, ktaps * chans),
-        (ktaps * chans, 5 * chans),
-        ((ktaps + 5) * chans, 4 * chans),
-    ]
+    unit = 2 * chans
+    streams = [(n * unit, unit) for n in range((ntaps + ktaps) // 2)]
+    chips = sizes["tm"] // 2
     core = [("tm", 0)]
-    chips = [("tm", b) for b in bits_of(sizes["tm"])[1:]]
     space = [("space", b) for b in bits_of(sizes["space"])]
     samp = [("samples", b) for b in bits_of(sizes["samples"])]
-    orders = [
-        core + samp + space + chips,
-        core + space + samp + chips,
-        core + samp + space + chips,
-    ]
-    steps_of, buffer_rows = plan(streams, orders)
-    most = max(len(steps) for steps in steps_of)
+    orders = [core + (space + samp if n % 2 else samp + space) for n in range(len(streams))]
+    steps_of, buffer_rows = plan(streams, orders, ("tm", 1, chips))
+    most = max(len(steps) for steps in steps_of) + chips - 1
     rows_all = (ntaps + ktaps) * chans
     tile = (height, wide, chans)
     sem = pltpu.SemaphoreType.DMA
     any_spec = pl.BlockSpec(memory_space=pl.ANY)
-    vmem_spec = pl.BlockSpec(memory_space=pltpu.VMEM)
-    block, fg, grads = pl.pallas_call(
-        functools.partial(kernel, sizes, streams, steps_of),
+    block, fg, sgrad, tgrad = pl.pallas_call(
+        functools.partial(kernel, sizes, streams, steps_of, chips),
         out_shape=(
             jax.ShapeDtypeStruct((samples * frames,) + tile, BF16),
             jax.ShapeDtypeStruct((samples * frames,) + tile, BF16),
-            jax.ShapeDtypeStruct((rows_all, chans), BF16),
+            jax.ShapeDtypeStruct((ntaps * chans, chans), BF16),
+            jax.ShapeDtypeStruct((ktaps * chans, chans), BF16),
         ),
         in_specs=[any_spec] * 4,
-        out_specs=(vmem_spec, vmem_spec, vmem_spec),
+        out_specs=(any_spec,) * 4,
         scratch_shapes=[
             pltpu.VMEM((frames,) + tile, BF16),
             pltpu.VMEM((frames, height + 2, wide, 3 * chans), BF16),
@@ -412,8 +500,11 @@
             pltpu.VMEM((rows_all, chans), BF16),
             pltpu.VMEM((buffer_rows, chans), BF16),
             pltpu.VMEM((buffer_rows, chans), BF16),
-            sem((4,)), sem((4,)), sem((4,)), sem((4,)), sem((4,)),
-            sem((3, most)), sem((3, most)), sem((3, most)), sem((3, most)),
+            pltpu.VMEM((2, frames) + tile, BF16),
+            sem((4,)), sem((2 * len(streams) + 3 * frames,)),
+            sem((4,)), sem((4,)), sem((4,)), sem((4,)),
+            sem((len(streams), most)), sem((len(streams), most)),
+            sem((len(streams), most)), sem((len(streams), most)),
         ],
         compiler_params=pltpu.CompilerParams(
             collective_id=0, has_side_effects=True, vmem_limit_bytes=60 * 1024 * 1024
@@ -426,12 +517,11 @@
     )
     devices = sizes["tm"] * sizes["space"] * sizes["samples"]
     factor = (samples * frames * height * wide * devices) ** (-0.5)
-    scaled = grads.astype(F32) * factor
     return (
         block.reshape(fields.shape),
         fg.reshape(fields.shape),
-        scaled[ktaps * chans :].reshape(spatial_weight.shape),
-        scaled[: ktaps * chans].reshape(temporal_weight.shape),
+        sgrad.astype(F32).reshape(spatial_weight.shape) * factor,
+        tgrad.astype(F32).reshape(temporal_weight.shape) * factor,
     )
 
 

time: 71.4 us -> 72.3 us (1.013)
  other arithmetic: 1.74 us -> 4.04 us
  local copies, waits for them, and re-layouts: 4.66 us -> 2.5 us
  Pallas kernels: 64.1 us -> 65 us
    slice x2 -> x0, local copies, waits for them, and re-layouts: 2.7 us -> none  [the longest x1 1.56 us: shards(): scaled[ktaps * chans:].reshape(spatial_weight.shape)]
    mul x1 -> x2, other arithmetic: 1.74 us -> 4.04 us  [the longest x1 2.89 us: shards(): sgrad.astype(F32).reshape(spatial_weight.shape) * factor]
    pallas_call x1, Pallas kernels: 64.1 us -> 65 us  [shards(): pl.pallas_call(functools.partial(kernel, sizes, streams, steps_of, chips)...]
    unnamed x6 -> x8, local copies, waits for them, and re-layouts: 1.96 us -> 2.5 us
where the time goes in v2:
time: 72.3 us; the launch traced here: 72.2 us
  Pallas kernels  65 us (90%)
  other arithmetic  4.04 us (6%)
  local copies, waits for them, and re-layouts  2.5 us (3%)
    pallas_call x1, Pallas kernels, shards(): pl.pallas_call(functools.partial(kernel, sizes, streams, steps_of, chips)...  65 us
    mul x1, other arithmetic, shards(): sgrad.astype(F32).reshape(spatial_weight.shape) * factor  2.89 us
    unnamed x8, local copies, waits for them, and re-layouts  2.5 us

profile of v2, /device:TPU:0, one launch (start us, length us, event | category | flops | bytes accessed | tf_op | source)
XLA Modules:
  0.0 72.2 jit_solution(1634656795735583067)
XLA Ops:
  0.6 65.0 %shard_map.75 = (bf16[2,8,128,256]{3,2,1,0:T(8,128)(2,1)}, bf16[2,8,128,256]{3,2,1,0:T(8,128)(2,1)}, bf16[2304,256]{1,0:T(8,128)(2,1)}, bf16[1280,256]{1,0:T(8,128)(2,1)}) custom-call(bf16[2,8,128,256]{3,2,1,0:T(8,128)(2,1)} %bitcast.13, bf16[2,8,128,256]{3,2,1,0:T(8,128)(2,1)} %bitcast.14, bf16[2304,256]{1,0:T(8,128)(2,1)} %bitcast.10, ...), custom_call_target="tpu_custom_call" | custom-call | tf_op jit(solution)/shard_map/pallas_call | solution.py:473
  65.6 0.0 copy-start.2
  65.6 2.9 %convert_multiply_fusion = f32[2304,256]{1,0:T(8,128)} fusion(bf16[2304,256]{1,0:T(8,128)(2,1)} %get-tuple-element.10), kind=kLoop, calls=%fused_computation | loop fusion | flops 1179648 | bytes 3538944 | tf_op jit(solution)/shard_map/mul | solution.py:523
  68.5 0.0 copy-start.1
  68.5 0.0 copy-done.2
  68.5 1.1 %convert_multiply_fusion.1 = f32[1280,256]{1,0:T(8,128)} fusion(bf16[1280,256]{1,0:T(8,128)(2,1)S(1)} %copy-done.2), kind=kLoop, calls=%fused_computation.1 | loop fusion | flops 655360 | bytes 1966080 | tf_op jit(solution)/shard_map/mul | solution.py:524
  69.7 0.0 copy-start
  69.7 0.5 copy-done.1
  70.2 1.0 %copy.10 = bf16[1,2,8,128,256]{4,3,2,1,0:T(8,128)(2,1)} copy(bf16[1,2,8,128,256]{4,3,2,1,0:T(8,128)(2,1)S(1)} %bitcast.12) | data formatting | bytes 2097152
  71.2 0.0 copy-done
  71.2 1.0 %copy.11 = bf16[1,2,8,128,256]{4,3,2,1,0:T(8,128)(2,1)} copy(bf16[1,2,8,128,256]{4,3,2,1,0:T(8,128)(2,1)S(1)} %bitcast.11) | data formatting | bytes 2097152
Async XLA Ops:
  65.6 2.9 %copy-start.2 = (bf16[1280,256]{1,0:T(8,128)(2,1)S(1)}, bf16[1280,256]{1,0:T(8,128)(2,1)}, u32[]{:S(2)}) copy-start(bf16[1280,256]{1,0:T(8,128)(2,1)} %get-tuple-element.11) | copy-start | bytes 1966084
  68.5 1.7 %copy-start.1 = (bf16[2,8,128,256]{3,2,1,0:T(8,128)(2,1)S(1)}, bf16[2,8,128,256]{3,2,1,0:T(8,128)(2,1)}, u32[]{:S(2)}) copy-start(bf16[2,8,128,256]{3,2,1,0:T(8,128)(2,1)} %get-tuple-element.8) | copy-start | bytes 3145732
  69.7 1.5 %copy-start = (bf16[2,8,128,256]{3,2,1,0:T(8,128)(2,1)S(1)}, bf16[2,8,128,256]{3,2,1,0:T(8,128)(2,1)}, u32[]{:S(2)}) copy-start(bf16[2,8,128,256]{3,2,1,0:T(8,128)(2,1)} %get-tuple-element.9) | copy-start | bytes 3145732

commit v3 on v2

--- a/solution.py
+++ b/solution.py
@@ -420,8 +420,11 @@
         for side in range(2):
             spread(hghalo[side, f], hgs, f, side * (height + 1))
 
+    rounds = []
+
     def round_of_moves():
-        advance(*range(len(queues)))
+        advance(*range(2 if len(rounds) < 3 else 0, len(queues)))
+        rounds.append(0)
 
     done = []
 

time: 72.3 us -> 72.6 us (level)
  no operation moved by 1% of the time
where the time goes in v3:
time: 72.6 us; the launch traced here: 72.4 us
  Pallas kernels  65.2 us (90%)
  other arithmetic  4.04 us (6%)
  local copies, waits for them, and re-layouts  2.5 us (3%)
    pallas_call x1, Pallas kernels, shards(): pl.pallas_call(functools.partial(kernel, sizes, streams, steps_of, chips)...  65.2 us
    mul x1, other arithmetic, shards(): sgrad.astype(F32).reshape(spatial_weight.shape) * factor  2.89 us
    unnamed x8, local copies, waits for them, and re-layouts  2.5 us

profile of v3, /device:TPU:0, one launch (start us, length us, event | category | flops | bytes accessed | tf_op | source)
XLA Modules:
  0.0 72.4 jit_solution(5244605667649587069)
XLA Ops:
  0.6 65.2 %shard_map.75 = (bf16[2,8,128,256]{3,2,1,0:T(8,128)(2,1)}, bf16[2,8,128,256]{3,2,1,0:T(8,128)(2,1)}, bf16[2304,256]{1,0:T(8,128)(2,1)}, bf16[1280,256]{1,0:T(8,128)(2,1)}) custom-call(bf16[2,8,128,256]{3,2,1,0:T(8,128)(2,1)} %bitcast.13, bf16[2,8,128,256]{3,2,1,0:T(8,128)(2,1)} %bitcast.14, bf16[2304,256]{1,0:T(8,128)(2,1)} %bitcast.10, ...), custom_call_target="tpu_custom_call" | custom-call | tf_op jit(solution)/shard_map/pallas_call | solution.py:476
  65.9 0.0 copy-start.2
  65.9 2.9 %convert_multiply_fusion = f32[2304,256]{1,0:T(8,128)} fusion(bf16[2304,256]{1,0:T(8,128)(2,1)} %get-tuple-element.10), kind=kLoop, calls=%fused_computation | loop fusion | flops 1179648 | bytes 3538944 | tf_op jit(solution)/shard_map/mul | solution.py:526
  68.8 0.0 copy-start.1
  68.8 0.0 copy-done.2
  68.8 1.1 %convert_multiply_fusion.1 = f32[1280,256]{1,0:T(8,128)} fusion(bf16[1280,256]{1,0:T(8,128)(2,1)S(1)} %copy-done.2), kind=kLoop, calls=%fused_computation.1 | loop fusion | flops 655360 | bytes 1966080 | tf_op jit(solution)/shard_map/mul | solution.py:527
  69.9 0.0 copy-start
  69.9 0.5 copy-done.1
  70.5 1.0 %copy.10 = bf16[1,2,8,128,256]{4,3,2,1,0:T(8,128)(2,1)} copy(bf16[1,2,8,128,256]{4,3,2,1,0:T(8,128)(2,1)S(1)} %bitcast.12) | data formatting | bytes 2097152
  71.4 0.0 copy-done
  71.4 1.0 %copy.11 = bf16[1,2,8,128,256]{4,3,2,1,0:T(8,128)(2,1)} copy(bf16[1,2,8,128,256]{4,3,2,1,0:T(8,128)(2,1)S(1)} %bitcast.11) | data formatting | bytes 2097152
Async XLA Ops:
  65.9 2.9 %copy-start.2 = (bf16[1280,256]{1,0:T(8,128)(2,1)S(1)}, bf16[1280,256]{1,0:T(8,128)(2,1)}, u32[]{:S(2)}) copy-start(bf16[1280,256]{1,0:T(8,128)(2,1)} %get-tuple-element.11) | copy-start | bytes 1966084
  68.8 1.7 %copy-start.1 = (bf16[2,8,128,256]{3,2,1,0:T(8,128)(2,1)S(1)}, bf16[2,8,128,256]{3,2,1,0:T(8,128)(2,1)}, u32[]{:S(2)}) copy-start(bf16[2,8,128,256]{3,2,1,0:T(8,128)(2,1)} %get-tuple-element.8) | copy-start | bytes 3145732
  69.9 1.5 %copy-start = (bf16[2,8,128,256]{3,2,1,0:T(8,128)(2,1)S(1)}, bf16[2,8,128,256]{3,2,1,0:T(8,128)(2,1)}, u32[]{:S(2)}) copy-start(bf16[2,8,128,256]{3,2,1,0:T(8,128)(2,1)} %get-tuple-element.9) | copy-start | bytes 3145732
